TPU v7x, 32 devices: a whole 2x2x4 slice. The times are simulated.
32 devices in a mesh: dp: 16 (over z, y, core), tensor: 2 (over x).
Axes of the slice: x: 2, y: 2, z: 4, core: 2. Of those that a mesh axis runs over, the one named last changes fastest.
Arguments:
- tokens: bfloat16 [16384, 768], P(('dp', 'tensor')), may hold values from -6 to 6
- query_weight: bfloat16 [768, 768], P('dp', 'tensor'), may hold values from -0.21875 to 0.21875
- query_bias: float32 [768], replicated, may hold values from -3 to 3
- key_weight: bfloat16 [768, 768], P('dp', 'tensor'), may hold values from -0.21875 to 0.21875
- value_weight: bfloat16 [768, 768], P('dp', 'tensor'), may hold values from -0.21875 to 0.21875
- value_bias: float32 [768], replicated, may hold values from -0.625 to 0.625
- output_weight: bfloat16 [768, 768], P('tensor', 'dp'), may hold values from -1.25 to 1.25
- output_bias: float32 [768], replicated, may hold values from -3 to 3
- first_gain: float32 [768], replicated, may hold values from 0.5 to 1.5
- first_shift: float32 [768], replicated, may hold values from -3 to 3
- inner_weight: bfloat16 [768, 3072], P('dp', 'tensor'), may hold values from -0.21875 to 0.21875
- inner_bias: float32 [3072], replicated, may hold values from -3 to 3
- outer_weight: bfloat16 [3072, 768], P('tensor', 'dp'), may hold values from -0.109375 to 0.109375
- outer_bias: float32 [768], replicated, may hold values from -3 to 3
- second_gain: float32 [768], replicated, may hold values from 0.5 to 1.5
- second_shift: float32 [768], replicated, may hold values from -3 to 3
- segments: int32 [16, 1024], P('dp'), may hold values from 0 to 7, never falling along the last dimension, each value on 1 to 768 neighbouring positions
- valid_length: int32 [16], P('dp'), may hold values from 512 to 1024
- cotangent: bfloat16 [16384, 768], P(('dp', 'tensor')), may hold values from -6 to 6
Outputs:
- layer_output: bfloat16 [16384, 768], P(('dp', 'tensor'))
- input_gradient: float32 [16384, 768], P(('dp', 'tensor'))
- query_weight_gradient: float32 [768, 768], P('dp', 'tensor')
- query_bias_gradient: float32 [768], replicated
- key_weight_gradient: float32 [768, 768], P('dp', 'tensor')
- value_weight_gradient: float32 [768, 768], P('dp', 'tensor')
- value_bias_gradient: float32 [768], replicated
- output_weight_gradient: float32 [768, 768], P('tensor', 'dp')
- output_bias_gradient: float32 [768], replicated
- first_gain_gradient: float32 [768], replicated
- first_shift_gradient: float32 [768], replicated
- inner_weight_gradient: float32 [768, 3072], P('dp', 'tensor')
- inner_bias_gradient: float32 [3072], replicated
- outer_weight_gradient: float32 [3072, 768], P('tensor', 'dp')
- outer_bias_gradient: float32 [768], replicated
- second_gain_gradient: float32 [768], replicated
- second_shift_gradient: float32 [768], replicated
Inputs may be any that keep to these rules, and one draw needn't show every extreme that they name: `segments`: segment numbers never fall along a sequence; a token attends only to tokens of its own document. tokens of a sequence at positions valid_length and beyond are padding: no query attends to them as keys except the token itself.
All inputs are finite; a program needn't handle non-finite values.
Results may differ from a plain program's by a relative error of at most 0.013.
Values may be sent and summed in bfloat16 or wider, within the bound.
No kernel may reach another device: no remote copies, remote signals or barrier semaphores. Data moves between devices by JAX's collectives and lax.ppermute only.
A program may use at most 128 MiB of HBM per device.

v0:
```python
import jax
import jax.numpy as jnp
from jax import lax
from jax.sharding import PartitionSpec as P

HEAD_DIM = 64
norm_epsilon = 1e-12
masked_score = -1e30


def normalize(matrix, gain, shift):
    center = matrix - jnp.mean(matrix, axis=-1, keepdims=True)
    spread = jnp.mean(center * center, axis=-1, keepdims=True)
    return center * lax.rsqrt(spread + norm_epsilon) * gain + shift


def block_scores(query_block, key_seq, segment_row, valid_count, first_row):
    block_rows = query_block.shape[0]
    length = key_seq.shape[0]
    scores = (
        jnp.einsum("qhd,khd->hqk", query_block, key_seq, preferred_element_type=jnp.float32) * 0.125
    )
    positions = jnp.arange(length, dtype=jnp.int32)
    query_pos = first_row + jnp.arange(block_rows, dtype=jnp.int32)
    query_seg = lax.dynamic_slice_in_dim(segment_row, first_row, block_rows)
    allowed = (query_seg[:, None] == segment_row[None, :]) & (
        (positions[None, :] < valid_count) | (query_pos[:, None] == positions[None, :])
    )
    return jnp.where(allowed[None], scores, masked_score)


def attend_sequence(pieces):
    query_seq, key_seq, value_seq, segment_row, valid_count = pieces
    length = query_seq.shape[0]
    block_rows = min(512, length)

    def one_block(block_index):
        first_row = block_index * block_rows
        query_block = lax.dynamic_slice_in_dim(query_seq, first_row, block_rows)
        masked = block_scores(query_block, key_seq, segment_row, valid_count, first_row)
        largest = jnp.max(masked, axis=-1, keepdims=True)
        totals = jnp.sum(jnp.exp(masked - largest), axis=-1, keepdims=True)
        log_total = largest + jnp.log(totals)
        probs_low = jnp.exp(masked - log_total).astype(jnp.bfloat16)
        context = jnp.einsum(
            "hqk,khd->qhd", probs_low, value_seq, preferred_element_type=jnp.float32
        )
        return (context.astype(jnp.bfloat16), log_total[..., 0])

    contexts, log_totals = lax.map(one_block, jnp.arange(length // block_rows, dtype=jnp.int32))
    return (contexts.reshape(query_seq.shape), log_totals)


def attend_backward(pieces):
    query_seq, key_seq, value_seq, segment_row, valid_count, grad_seq, log_totals = pieces
    length = query_seq.shape[0]
    block_rows = min(512, length)

    def one_block(running, inputs):
        key_grad, value_grad = running
        block_index, log_total = inputs
        first_row = block_index * block_rows
        query_block = lax.dynamic_slice_in_dim(query_seq, first_row, block_rows)
        grad_block = lax.dynamic_slice_in_dim(grad_seq, first_row, block_rows)
        masked = block_scores(query_block, key_seq, segment_row, valid_count, first_row)
        probs = jnp.exp(masked - log_total[..., None])
        probs_low = probs.astype(jnp.bfloat16)
        value_grad = value_grad + jnp.einsum(
            "hqk,qhd->khd", probs_low, grad_block, preferred_element_type=jnp.float32
        )
        d_probs = jnp.einsum(
            "qhd,khd->hqk", grad_block, value_seq, preferred_element_type=jnp.float32
        )
        row_inner = jnp.sum(probs * d_probs, axis=-1, keepdims=True)
        d_scores = (probs * (d_probs - row_inner)).astype(jnp.bfloat16)
        query_grad = (
            jnp.einsum("hqk,khd->qhd", d_scores, key_seq, preferred_element_type=jnp.float32)
            * 0.125
        )
        key_grad = (
            key_grad
            + jnp.einsum("hqk,qhd->khd", d_scores, query_block, preferred_element_type=jnp.float32)
            * 0.125
        )
        return ((key_grad, value_grad), query_grad.astype(jnp.bfloat16))

    empty = jnp.zeros(key_seq.shape, jnp.float32)
    block_ids = jnp.arange(length // block_rows, dtype=jnp.int32)
    (key_grad, value_grad), query_grads = lax.scan(
        one_block, (empty, empty), (block_ids, log_totals)
    )
    return (
        query_grads.reshape(query_seq.shape),
        key_grad.astype(jnp.bfloat16),
        value_grad.astype(jnp.bfloat16),
    )


def slope_and_gelu(inner):
    rise = 0.5 * (1.0 + lax.erf(inner * 0.7071067811865476))
    density = jnp.exp(-0.5 * inner * inner) * 0.3989422804014327
    return (inner * rise, rise + inner * density)


def norm_backward(matrix, gain, grad):
    center = matrix - jnp.mean(matrix, axis=-1, keepdims=True)
    spread = jnp.mean(center * center, axis=-1, keepdims=True)
    scale = lax.rsqrt(spread + norm_epsilon)
    normed = center * scale
    d_normed = grad * gain
    pulled = scale * (
        d_normed
        - jnp.mean(d_normed, axis=-1, keepdims=True)
        - normed * jnp.mean(d_normed * normed, axis=-1, keepdims=True)
    )
    return (pulled, jnp.sum(grad * normed, axis=0), jnp.sum(grad, axis=0))


def halves_in_order(mine, other, shard_index):
    first = shard_index == 0
    return (jnp.where(first, mine, other), jnp.where(first, other, mine))


def mix(left, right, dims):
    return lax.dot_general(left, right, (dims, ((), ())), preferred_element_type=jnp.float32)


def on_device(
    tokens,
    query_weight,
    query_bias,
    key_weight,
    value_weight,
    value_bias,
    output_weight,
    output_bias,
    first_gain,
    first_shift,
    inner_weight,
    inner_bias,
    outer_weight,
    outer_bias,
    second_gain,
    second_shift,
    segments,
    valid_length,
    cotangent,
):
    low = jnp.bfloat16
    whole = ("tensor", "dp")
    swap = [(0, 1), (1, 0)]
    own_rows, width = tokens.shape
    head_cols = query_weight.shape[1]
    hidden_cols = inner_weight.shape[1]
    local_heads = head_cols // HEAD_DIM
    shard_index = lax.axis_index("tensor")
    own_start = shard_index * own_rows
    other_start = (1 - shard_index) * own_rows
    other_tokens = lax.ppermute(tokens, "tensor", swap)
    full_qkv = lax.all_gather(
        jnp.concatenate([query_weight, key_weight, value_weight], axis=1), "dp", axis=0, tiled=True
    )
    full_output = lax.all_gather(output_weight.T, whole, axis=0, tiled=True)
    full_inner = lax.all_gather(inner_weight, whole, axis=0, tiled=True)
    full_outer = lax.all_gather(outer_weight.T, whole, axis=0, tiled=True)
    full_output = full_output.reshape(2, width, head_cols)
    full_inner = full_inner.reshape(2, width, hidden_cols)
    full_outer = full_outer.reshape(2, width, hidden_cols)
    group_rows = jnp.concatenate(halves_in_order(tokens, other_tokens, shard_index), axis=0)
    bias_query = lax.dynamic_slice_in_dim(query_bias, shard_index * head_cols, head_cols)
    bias_value = lax.dynamic_slice_in_dim(value_bias, shard_index * head_cols, head_cols)
    bias_qkv = jnp.concatenate([bias_query, jnp.zeros_like(bias_query), bias_value])
    seq_count, seq_length = segments.shape
    four_shape = (seq_count, seq_length, local_heads, HEAD_DIM)
    qkv = (mix(group_rows, full_qkv, ((1,), (0,))) + bias_qkv).astype(low)
    queries = qkv[:, :head_cols].reshape(four_shape)
    keys_all = qkv[:, head_cols : 2 * head_cols].reshape(four_shape)
    values_all = qkv[:, 2 * head_cols :].reshape(four_shape)
    contexts, log_totals = lax.map(
        attend_sequence, (queries, keys_all, values_all, segments, valid_length)
    )
    context = contexts.reshape(seq_count * seq_length, head_cols)
    own_context = lax.dynamic_slice_in_dim(context, own_start, own_rows)
    far_context = lax.ppermute(
        lax.dynamic_slice_in_dim(context, other_start, own_rows), "tensor", swap
    )
    context_halves = halves_in_order(own_context, far_context, shard_index)
    attended = mix(context_halves[0], full_output[0], ((1,), (1,))) + mix(
        context_halves[1], full_output[1], ((1,), (1,))
    )
    first_sum = tokens.astype(jnp.float32) + attended + output_bias
    hidden = normalize(first_sum, first_gain, first_shift)
    hidden_low = hidden.astype(low)
    activated, slopes = ([], [])
    outer = outer_bias
    for half in range(2):
        inner = (
            mix(hidden_low, full_inner[half], ((1,), (0,)))
            + inner_bias[half * hidden_cols : (half + 1) * hidden_cols]
        )
        value, slope = slope_and_gelu(inner)
        activated.append(value.astype(low))
        slopes.append(slope)
        outer = outer + mix(activated[half], full_outer[half], ((1,), (1,)))
    second_sum = hidden + outer
    layer_output = normalize(second_sum, second_gain, second_shift).astype(low)
    d_second, second_gain_grad, second_shift_grad = norm_backward(
        second_sum, second_gain, cotangent.astype(jnp.float32)
    )
    outer_bias_grad = jnp.sum(d_second, axis=0)
    d_outer = d_second.astype(low)
    outer_weight_grad = jnp.stack(
        [mix(d_outer, activated[half], ((0,), (0,))).astype(low) for half in range(2)]
    )
    d_hidden = d_second
    inner_grads, inner_bias_parts = ([], [])
    for half in range(2):
        d_activated = mix(d_outer, full_outer[half], ((1,), (0,)))
        d_inner = (d_activated * slopes[half]).astype(low)
        inner_grads.append(mix(hidden_low, d_inner, ((0,), (0,))).astype(low))
        inner_bias_parts.append(jnp.sum(d_inner, axis=0, dtype=jnp.float32))
        d_hidden = d_hidden + mix(d_inner, full_inner[half], ((1,), (1,)))
    inner_weight_grad = jnp.stack(inner_grads)
    inner_bias_grad = jnp.concatenate(inner_bias_parts)
    d_first, first_gain_grad, first_shift_grad = norm_backward(first_sum, first_gain, d_hidden)
    output_bias_grad = jnp.sum(d_first, axis=0)
    d_attended = d_first.astype(low)
    output_weight_grad = jnp.stack(
        [mix(d_attended, context_halves[half], ((0,), (0,))).astype(low) for half in range(2)]
    )
    d_context_halves = [
        mix(d_attended, full_output[half], ((1,), (0,))).astype(low) for half in range(2)
    ]
    first = shard_index == 0
    own_d_context = jnp.where(first, d_context_halves[0], d_context_halves[1])
    far_d_context = lax.ppermute(
        jnp.where(first, d_context_halves[1], d_context_halves[0]), "tensor", swap
    )
    d_context = jnp.concatenate(halves_in_order(own_d_context, far_d_context, shard_index), axis=0)
    d_queries, d_keys, d_values = lax.map(
        attend_backward,
        (
            queries,
            keys_all,
            values_all,
            segments,
            valid_length,
            d_context.reshape(four_shape),
            log_totals,
        ),
    )
    flat = (seq_count * seq_length, head_cols)
    d_qkv = jnp.concatenate(
        [d_queries.reshape(flat), d_keys.reshape(flat), d_values.reshape(flat)], axis=1
    )
    qkv_weight_grad = mix(group_rows, d_qkv, ((0,), (0,))).astype(low)
    partial_input = mix(d_qkv, full_qkv, ((1,), (1,)))
    far_input = lax.ppermute(
        lax.dynamic_slice_in_dim(partial_input, other_start, own_rows).astype(low), "tensor", swap
    )
    input_gradient = (
        d_first
        + lax.dynamic_slice_in_dim(partial_input, own_start, own_rows)
        + far_input.astype(jnp.float32)
    )

    def scatter(partial, axes):
        return lax.psum_scatter(
            partial.reshape(-1, partial.shape[-1]), axes, scatter_dimension=0, tiled=True
        ).astype(jnp.float32)

    outer_shard = scatter(outer_weight_grad, whole).T
    inner_shard = scatter(inner_weight_grad, whole)
    output_shard = scatter(output_weight_grad, whole).T
    qkv_shard = scatter(qkv_weight_grad, ("dp",))
    bias_local = jnp.sum(d_qkv, axis=0, dtype=jnp.float32)
    spread_out = lax.dynamic_update_slice(
        jnp.zeros((2, width), jnp.float32),
        jnp.stack([bias_local[:head_cols], bias_local[2 * head_cols :]]),
        (0, shard_index * head_cols),
    )
    pieces = [
        spread_out.reshape(-1),
        output_bias_grad,
        first_gain_grad,
        first_shift_grad,
        outer_bias_grad,
        second_gain_grad,
        second_shift_grad,
        inner_bias_grad,
    ]
    summed = lax.psum(jnp.concatenate(pieces), ("dp", "tensor"))
    rows = summed[: 8 * width].reshape(8, width)
    return (
        layer_output,
        input_gradient,
        qkv_shard[:, :head_cols],
        rows[0],
        qkv_shard[:, head_cols : 2 * head_cols],
        qkv_shard[:, 2 * head_cols :],
        rows[1],
        output_shard,
        rows[2],
        rows[3],
        rows[4],
        inner_shard,
        summed[8 * width :],
        outer_shard,
        rows[5],
        rows[6],
        rows[7],
    )


def solution(mesh):
    placed = (
        P(("dp", "tensor"), None),
        P("dp", "tensor"),
        P(),
        P("dp", "tensor"),
        P("dp", "tensor"),
        P(),
        P("tensor", "dp"),
        P(),
        P(),
        P(),
        P("dp", "tensor"),
        P(),
        P("tensor", "dp"),
        P(),
        P(),
        P(),
        P("dp", None),
        P("dp"),
        P(("dp", "tensor"), None),
    )
    return jax.shard_map(
        on_device,
        mesh=mesh,
        in_specs=placed,
        out_specs=(
            P(("dp", "tensor"), None),
            P(("dp", "tensor"), None),
            P("dp", "tensor"),
            P(),
            P("dp", "tensor"),
            P("dp", "tensor"),
            P(),
            P("tensor", "dp"),
            P(),
            P(),
            P(),
            P("dp", "tensor"),
            P(),
            P("tensor", "dp"),
            P(),
            P(),
            P(),
        ),
        check_vma=False,
    )
```

profile of v0, /device:TPU:0, one launch (start us, length us, event | category | flops | bytes accessed | tf_op | source)
XLA Modules:
  0.0 660.5 jit_solution(15233943400228055662)
XLA Ops:
  10.3 3.0 collective-permute-start
  14.9 16.1 %collective-permute-done = bf16[512,768]{1,0:T(8,128)(2,1)S(1)} collective-permute-done((bf16[512,768]{1,0:T(8,128)(2,1)}, bf16[512,768]{1,0:T(8,128)(2,1)S(1)}, u32[]{:S(2)}, u32[]{:S(2)}) %collective-permute-start) | collective-permute-done | bytes 786464 | tf_op jit(solution)/shard_map/ppermute | solution.py:159
  32.3 21.4 %all-gather.5.cloned.1.call-done = bf16[768,1152]{1,0:T(8,128)(2,1)} async-done(((bf16[48,1152]{1,0:T(8,128)(2,1)}), bf16[768,1152]{1,0:T(8,128)(2,1)}) %all-gather.5.cloned.1.call-update) | async-done | bytes 1769488 | tf_op jit(solution)/shard_map/all_gather | solution.py:160
  53.7 3.7 add_convert_fusion
  58.6 35.0 %while.47 = (s32[]{:T(128)}, bf16[2,512,6,64]{1,3,2,0:T(8,128)(2,1)S(1)}, f32[2,6,512]{2,1,0:T(8,128)S(1)}, s32[2]{0:T(128)S(1)}, s32[1024]{0:T(1024)S(1)}, /*in...) while((s32[]{:T(128)}, ...), condition=%wide.region_3.4_spmd, body=%wide.region_0.3_spmd.sunk | while | flops 842201600 | bytes 92672224 | solution.py:50
  61.4 2.4 fusion.143
  63.9 3.7 exponential_reduce_fusion.2
  68.4 7.8 %fusion.144 = bf16[2,512,6,64]{1,3,2,0:T(8,128)(2,1)S(1)} fusion(bf16[2,512,6,64]{1,3,2,0:T(8,128)(2,1)S(1)} %get-tuple-element.507, s32[]{:T(128)} %get-tuple-element.506, bf16[1024,6,64]{0,2,1:T(8,128)(2,1)S(1)} %get-tuple-element.527, f32[6,512,1024]{2,1,0:T(8,128)} %copy-done.2, f32[6,512]{1,0:T(8,128)S(1)} %get-tuple-element.477, ...), kind=kOutput, calls=%fused_computation.11.clone.1 | convolution fusion | flops 415432704 | bytes 14303236 | tf_op jit(solution)/shard_map/while/body/eval_jaxpr/while/body/eval_jaxpr/hqk,khd->qhd/dot_general | solution.py:45
  78.8 2.4 fusion.143
  81.3 3.7 exponential_reduce_fusion.2
  85.8 7.8 %fusion.144 = bf16[2,512,6,64]{1,3,2,0:T(8,128)(2,1)S(1)} fusion(bf16[2,512,6,64]{1,3,2,0:T(8,128)(2,1)S(1)} %get-tuple-element.507, s32[]{:T(128)} %get-tuple-element.506, bf16[1024,6,64]{0,2,1:T(8,128)(2,1)S(1)} %get-tuple-element.527, f32[6,512,1024]{2,1,0:T(8,128)} %copy-done.2, f32[6,512]{1,0:T(8,128)S(1)} %get-tuple-element.477, ...), kind=kOutput, calls=%fused_computation.11.clone.1 | convolution fusion | flops 415432704 | bytes 14303236 | tf_op jit(solution)/shard_map/while/body/eval_jaxpr/while/body/eval_jaxpr/hqk,khd->qhd/dot_general | solution.py:45
  95.5 1.9 copy.53
  100.2 9.4 %all-gather.7.cloned.1.call-done = bf16[1536,384]{1,0:T(8,128)(2,1)} async-done(((bf16[48,384]{1,0:T(8,128)(2,1)}), bf16[1536,384]{1,0:T(8,128)(2,1)}) %all-gather.7.cloned.1.call-update) | async-done | bytes 1179664 | tf_op jit(solution)/shard_map/all_gather | solution.py:163
  111.5 1.9 fusion.92
  115.8 60.4 %all-gather.9.cloned.1.call-done = bf16[1536,1536]{1,0:T(8,128)(2,1)} async-done(((bf16[48,1536]{1,0:T(8,128)(2,1)}), bf16[1536,1536]{1,0:T(8,128)(2,1)}) %all-gather.9.cloned.1.call-update) | async-done | bytes 4718608 | tf_op jit(solution)/shard_map/all_gather | solution.py:164
  176.2 5.8 multiply_convert_fusion.1
  182.0 3.5 multiply_convert_fusion.2
  185.5 55.4 %all-gather.11.cloned.1.call-done = bf16[1536,1536]{1,0:T(8,128)(2,1)} async-done(((bf16[48,1536]{1,0:T(8,128)(2,1)}), bf16[1536,1536]{1,0:T(8,128)(2,1)}) %all-gather.11.cloned.1.call-update) | async-done | bytes 4718608 | tf_op jit(solution)/shard_map/all_gather | solution.py:165
  240.9 3.7 fusion.54
  248.7 2.1 fusion.84
  250.9 3.2 convert_reduce_fusion.2
  254.1 3.2 convert_reduce_fusion.1
  258.7 2.3 multiply_reduce_fusion.1
  269.9 7.7 %collective-permute-done.2 = bf16[512,384]{1,0:T(8,128)(2,1)} collective-permute-done((bf16[512,384]{1,0:T(8,128)(2,1)}, bf16[512,384]{1,0:T(8,128)(2,1)}, u32[]{:S(2)}, u32[]{:S(2)}) %collective-permute-start.2) | collective-permute-done | bytes 393248 | tf_op jit(solution)/shard_map/ppermute | solution.py:236
  281.0 67.2 %while.48 = (s32[]{:T(128)}, f32[1024,6,64]{0,2,1:T(8,128)}, f32[1024,6,64]{0,2,1:T(8,128)}, bf16[2,512,6,64]{1,3,2,0:T(8,128)(2,1)}, s32[2]{0:T(128)S(1)}, /*in...) while((s32[]{:T(128)}, f32[1024,6,64]{0,2,1:T(8,128)}, ...), condition=%wide.region_14.15_spmd.clone, body=%wide.region_12.14_spmd.clone.sunk | while | flops 2064906752 | bytes 217293712 | solution.py:89
  284.1 1.8 fusion.154
  286.0 6.3 multiply_reduce_fusion.7
  292.3 5.1 multiply_convert_fusion.4
  297.4 5.4 bitcast_add_fusion.4
  302.7 6.4 fusion.156
  309.1 4.9 bitcast_add_fusion.5
  316.7 1.8 fusion.154
  318.6 6.3 multiply_reduce_fusion.7
  324.9 5.1 multiply_convert_fusion.4
  329.9 5.8 bitcast_add_fusion.4
  335.7 6.3 fusion.156
  342.0 6.0 bitcast_add_fusion.5
  348.2 2.1 copy.51
  352.3 3.5 convolution_convert_fusion.4
  355.9 2.9 fusion.46
  360.2 2.6 pad_maximum_fusion.1
  363.9 2.9 fusion.44
  368.3 2.6 pad_maximum_fusion
  371.5 3.8 fusion.83
  378.7 49.9 %psum.7 = f32[9216]{0:T(1024)S(1)} all-reduce(f32[9216]{0:T(1024)S(1)} %constant_dynamic-update-slice_fusion), channel_id=1, replica_groups=mesh['dp'=16,'tensor'=2] {'dp','tensor'}, use_global_device_ids=true, to_apply=%region_25.26 | all-reduce | flops 9216 | bytes 73728 | tf_op jit(solution)/shard_map/psum | solution.py:292
  429.8 2.8 convert_add_fusion
  435.5 103.8 %reduce-scatter.11.cloned.1.call-done = bf16[48,1536]{1,0:T(8,128)(2,1)} async-done(((bf16[1536,1536]{1,0:T(8,128)(2,1)}), bf16[48,1536]{1,0:T(8,128)(2,1)}) %reduce-scatter.11.cloned.1.call-update) | async-done | bytes 147472 | tf_op jit(solution)/shard_map/reduce_scatter | solution.py:268
  541.0 110.8 %reduce-scatter.9.cloned.1.call-done = bf16[48,1536]{1,0:T(8,128)(2,1)} async-done(((bf16[1536,1536]{1,0:T(8,128)(2,1)}), bf16[48,1536]{1,0:T(8,128)(2,1)}) %reduce-scatter.9.cloned.1.call-update) | async-done | bytes 147472 | tf_op jit(solution)/shard_map/reduce_scatter | solution.py:268
  (242 shorter events, 60.7 us)
Async XLA Ops:
  7.2 46.5 %all-gather.5.cloned.1.call-start = ((), (), s32[]{:S(2)}) async-start(), calls=%async_computation.4 | async-start | bytes 1880064 | tf_op jit(solution)/shard_map/all_gather | solution.py:160
  8.7 100.9 %all-gather.7.cloned.1.call-start = ((), (), s32[]{:S(2)}) async-start(), calls=%async_computation.5 | async-start | bytes 1216512 | tf_op jit(solution)/shard_map/all_gather | solution.py:163
  9.5 166.7 %all-gather.9.cloned.1.call-start = ((), (), s32[]{:S(2)}) async-start(), calls=%async_computation.6 | async-start | bytes 4866048 | tf_op jit(solution)/shard_map/all_gather | solution.py:164
  10.2 230.7 %all-gather.11.cloned.1.call-start = ((), (), s32[]{:S(2)}) async-start(), calls=%async_computation.7 | async-start | bytes 4866048 | tf_op jit(solution)/shard_map/all_gather | solution.py:165
  10.3 20.8 %collective-permute-start = (bf16[512,768]{1,0:T(8,128)(2,1)}, bf16[512,768]{1,0:T(8,128)(2,1)S(1)}, u32[]{:S(2)}, u32[]{:S(2)}) collective-permute-start(bf16[512,768]{1,0:T(8,128)(2,1)} %param.23), channel_id=1, source_target_pairs={{0,1},{1,0},{2,3},{3,2},{4,5},{5,4},{6,7},{7,6},{8,9},{9,8},{10,11... | collective-permute-start | bytes 2359304 | tf_op jit(solution)/shard_map/ppermute | solution.py:159
  13.3 419.3 %reduce-scatter.7.cloned.1.call-start = ((), (), s32[]{:S(2)}) async-start(), calls=%async_computation.9 | async-start | bytes 1216512 | tf_op jit(solution)/shard_map/reduce_scatter | solution.py:268
  32.3 21.4 %copy-start.20 = (bf16[512,768]{1,0:T(8,128)(2,1)}, bf16[512,768]{1,0:T(8,128)(2,1)S(1)}, u32[]{:S(2)}) copy-start(bf16[512,768]{1,0:T(8,128)(2,1)S(1)} %get-tuple-element.315) | copy-start | bytes 2359300
  32.3 21.4 %copy-start.22 = (bf16[512,768]{1,0:T(8,128)(2,1)}, bf16[512,768]{1,0:T(8,128)(2,1)S(1)}, u32[]{:S(2)}) copy-start(bf16[512,768]{1,0:T(8,128)(2,1)S(1)} %get-tuple-element.316) | copy-start | bytes 2359300
  63.8 4.5 copy-start.2
  81.3 4.5 copy-start.2
  94.4 4.6 copy-start.27
  95.5 15.9 %copy-start.39 = (f32[768]{0:T(1024)S(1)}, f32[768]{0:T(1024)}, u32[]{:S(2)}) copy-start(f32[768]{0:T(1024)} %param.30) | copy-start | bytes 9220
  97.4 12.2 %collective-permute-start.1 = (bf16[512,384]{1,0:T(8,128)(2,1)}, bf16[512,384]{1,0:T(8,128)(2,1)S(1)}, u32[]{:S(2)}, u32[]{:S(2)}) collective-permute-start(bf16[512,384]{1,0:T(8,128)(2,1)} %copy.53), channel_id=1, source_target_pairs={{0,1},{1,0},{2,3},{3,2},{4,5},{5,4},{6,7},{7,6},{8,9},{9,8},{10,11... | collective-permute-start | bytes 1179656 | tf_op jit(solution)/shard_map/ppermute | solution.py:184
  176.2 5.8 copy-start.16
  176.2 5.8 copy-start.41
  240.9 3.7 copy-start.7
  240.9 4.0 copy-start.42
  240.9 4.0 copy-start.43
  240.9 4.4 copy-start.50
  250.9 6.3 slice-start
  254.1 4.6 copy-start.44
  262.1 3.9 copy-start.8
  266.0 11.6 %collective-permute-start.2 = (bf16[512,384]{1,0:T(8,128)(2,1)}, bf16[512,384]{1,0:T(8,128)(2,1)}, u32[]{:S(2)}, u32[]{:S(2)}) collective-permute-start(bf16[512,384]{1,0:T(8,128)(2,1)} %get-tuple-element.345), channel_id=1, source_target_pairs={{0,1},{1,0},{2,3},{3,2},{4,5},{5,4},{6,7},{7,6},{8,9},{9,8},{10,11... | collective-permute-start | bytes 1179656 | tf_op jit(solution)/shard_map/ppermute | solution.py:236
  268.7 8.9 %copy-start.25 = (bf16[512,384]{1,0:T(8,128)(2,1)S(1)}, bf16[512,384]{1,0:T(8,128)(2,1)}, u32[]{:S(2)}) copy-start(bf16[512,384]{1,0:T(8,128)(2,1)} %copy-done.24) | copy-start | bytes 1179652
  268.7 8.9 %copy-start.26 = (bf16[512,384]{1,0:T(8,128)(2,1)S(1)}, bf16[512,384]{1,0:T(8,128)(2,1)}, u32[]{:S(2)}) copy-start(bf16[512,384]{1,0:T(8,128)(2,1)} %get-tuple-element.346) | copy-start | bytes 1179652
  269.9 164.2 %reduce-scatter.5.cloned.1.call-start = ((), (), s32[]{:S(2)}) async-start(), calls=%async_computation.8 | async-start | bytes 1880064 | tf_op jit(solution)/shard_map/reduce_scatter | solution.py:268
  281.4 4.6 copy-start.4
  286.0 6.3 copy-start
  297.4 11.7 %copy-start.1 = (f32[6,512,1024]{2,1,0:T(8,128)S(1)}, f32[6,512,1024]{2,1,0:T(8,128)}, u32[]{:S(2)}) copy-start(f32[6,512,1024]{2,1,0:T(8,128)} %copy-done) | copy-start | bytes 37748740 | tf_op jit(solution)/shard_map/while/body/eval_jaxpr/while
  302.7 6.4 copy-start.10
  309.1 4.9 copy-start.5
  314.0 4.6 copy-start.4
  318.6 6.3 copy-start
  329.9 12.1 %copy-start.1 = (f32[6,512,1024]{2,1,0:T(8,128)S(1)}, f32[6,512,1024]{2,1,0:T(8,128)}, u32[]{:S(2)}) copy-start(f32[6,512,1024]{2,1,0:T(8,128)} %copy-done) | copy-start | bytes 37748740 | tf_op jit(solution)/shard_map/while/body/eval_jaxpr/while
  335.7 6.3 copy-start.10
  342.0 6.1 copy-start.5
  355.8 183.6 %reduce-scatter.11.cloned.1.call-start = ((), (), s32[]{:S(2)}) async-start(), calls=%async_computation.11 | async-start | bytes 4866048 | tf_op jit(solution)/shard_map/reduce_scatter | solution.py:268
  362.8 289.0 %reduce-scatter.9.cloned.1.call-start = ((), (), s32[]{:S(2)}) async-start(), calls=%async_computation.10 | async-start | bytes 4866048 | tf_op jit(solution)/shard_map/reduce_scatter | solution.py:268
  371.4 7.1 %copy-start.31 = (f32[768]{0:T(1024)S(1)}, f32[768]{0:T(1024)}, u32[]{:S(2)}) copy-start(f32[768]{0:T(1024)} %get-tuple-element.305) | copy-start | bytes 9220
  371.4 7.1 %copy-start.38 = (f32[768]{0:T(1024)S(1)}, f32[768]{0:T(1024)}, u32[]{:S(2)}) copy-start(f32[768]{0:T(1024)} %get-tuple-element.251) | copy-start | bytes 9220
  371.4 7.1 %copy-start.37 = (f32[768]{0:T(1024)S(1)}, f32[768]{0:T(1024)}, u32[]{:S(2)}) copy-start(f32[768]{0:T(1024)} %get-tuple-element.256) | copy-start | bytes 9220
  371.4 7.1 %copy-start.33 = (f32[768]{0:T(1024)S(1)}, f32[768]{0:T(1024)}, u32[]{:S(2)}) copy-start(f32[768]{0:T(1024)} %get-tuple-element.303) | copy-start | bytes 9220
  371.4 7.1 %copy-start.30 = (f32[768]{0:T(1024)S(1)}, f32[768]{0:T(1024)}, u32[]{:S(2)}) copy-start(f32[768]{0:T(1024)} %get-tuple-element.253) | copy-start | bytes 9220
  371.4 7.1 %copy-start.29 = (f32[768]{0:T(1024)S(1)}, f32[768]{0:T(1024)}, u32[]{:S(2)}) copy-start(f32[768]{0:T(1024)} %get-tuple-element.258) | copy-start | bytes 9220
  371.5 7.2 %copy-start.34 = (f32[1536]{0:T(1024)S(1)}, f32[1536]{0:T(1024)}, u32[]{:S(2)}) copy-start(f32[1536]{0:T(1024)} %get-tuple-element.347) | copy-start | bytes 18436
  371.5 7.2 %copy-start.35 = (f32[1536]{0:T(1024)S(1)}, f32[1536]{0:T(1024)}, u32[]{:S(2)}) copy-start(f32[1536]{0:T(1024)} %get-tuple-element.349) | copy-start | bytes 18436
  376.9 52.9 %copy-start.9 = (f32[512,768]{1,0:T(8,128)S(1)}, f32[512,768]{1,0:T(8,128)}, u32[]{:S(2)}) copy-start(f32[512,768]{1,0:T(8,128)} %copy-done.8) | copy-start | bytes 4718596
  377.0 52.8 %collective-permute-start.3 = (bf16[512,768]{1,0:T(8,128)(2,1)S(1)}, bf16[512,768]{1,0:T(8,128)(2,1)S(1)}, u32[]{:S(2)}, u32[]{:S(2)}) collective-permute-start(bf16[512,768]{1,0:T(8,128)(2,1)S(1)} %dynamic-slice_convert_fusion), channel_id=1, source_target_pairs={{0,1},{1,0},{2,3},{3,2},{4,5},{5,4},{6,7},{7,6},{8,9},{9,8},{10,11... | collective-permute-start | bytes 2359304 | tf_op jit(solution)/shard_map/ppermute | solution.py:258
  (23 other events, 52.1 us)
Sparse Core Ops, SparseCore 0:
  10.7 42.8 all-gather.4
  56.6 53.0 all-gather.6
  112.6 63.5 all-gather.8
  179.0 61.8 all-gather.10
  270.0 95.4 reduce-scatter.6
  369.1 58.4 reduce-scatter.4
  433.0 106.2 reduce-scatter.10
  544.8 106.8 reduce-scatter.8
where the time goes:
time: 665 us; the launch traced here: 660 us
  waiting for transfers between devices  387 us (58%)
  matrix products  123 us (18%)
  blocking collectives  49.9 us (8%)
  other arithmetic  49.1 us (7%)
  local copies, waits for them, and re-layouts  25.9 us (4%)
  between operations  15.1 us (2%)
  starting transfers between devices  7.84 us (1%)
    reduce_scatter x4, waiting for transfers between devices, scatter(): lax.psum_scatter(partial.reshape(-1, partial.shape[-1]), axes, scatter_di...  215 us
    all_gather x1, waiting for transfers between devices, on_device(): full_inner = lax.all_gather(inner_weight, whole, axis=0, tiled=True)  60.4 us
    all_gather x1, waiting for transfers between devices, on_device(): full_outer = lax.all_gather(outer_weight.T, whole, axis=0, tiled=True)  55.4 us
    dot_general x21, matrix products, mix(): lax.dot_general(left, right, (dims, ((), ())), preferred_element_type=jnp...  51.2 us
    psum x1, blocking collectives, on_device(): summed = lax.psum(jnp.concatenate(pieces), ('dp', 'tensor'))  49.9 us
    all_gather x1, waiting for transfers between devices, on_device(): lax.all_gather(jnp.concatenate([query_weight, key_weight, value_weight],...  21.4 us
    ppermute x1, waiting for transfers between devices, on_device(): other_tokens = lax.ppermute(tokens, 'tensor', swap)  16.1 us
    dot_general x2, matrix products, one_block(): jnp.einsum('hqk,khd->qhd', probs_low, value_seq, preferred_element_type=j...  15.6 us
  transfers between devices with their start and end apart: 12, of which 8 were waited for; matrix products, arithmetic and copies ran while one was open for 25% of the time, Pallas kernels for 0%

commit v1 on v0

--- a/solution.py
+++ b/solution.py
@@ -289,7 +289,8 @@
         second_shift_grad,
         inner_bias_grad,
     ]
-    summed = lax.psum(jnp.concatenate(pieces), ("dp", "tensor"))
+    block_here = jnp.concatenate(pieces)
+    summed = jnp.sum(lax.all_gather(block_here, ("dp", "tensor")), axis=0)
     rows = summed[: 8 * width].reshape(8, width)
     return (
         layer_output,

time: 665 us -> 720 us (1.083)
  waiting for transfers between devices: 387 us -> 492 us
  blocking collectives: 49.9 us -> 0 us
    reduce_scatter x4, waiting for transfers between devices: 215 us -> 280 us  [scatter(): lax.psum_scatter(partial.reshape(-1, partial.shape[-1]), axes, scatter_di...]
    psum x1 -> x0, blocking collectives: 49.9 us -> none  [on_device(): summed = lax.psum(jnp.concatenate(pieces), ('dp', 'tensor'))]
    all_gather x0 -> x1, waiting for transfers between devices: none -> 21.7 us  [on_device(): summed = jnp.sum(lax.all_gather(block_here, ('dp', 'tensor')), axis=0)]
    ppermute x1, waiting for transfers between devices: 0.01 us -> 18.6 us  [on_device(): lax.ppermute(lax.dynamic_slice_in_dim(partial_input, other_start, own_row...]
  transfers between devices with their start and end apart: 12 -> 13, of which waited for: 8 -> 11; matrix products, arithmetic and copies ran while one was open for 25% -> 23% of each run, Pallas kernels for 0% -> 0%
where the time goes in v1:
time: 720 us; the launch traced here: 716 us
  waiting for transfers between devices  492 us (68%)
  matrix products  124 us (17%)
  other arithmetic  47.7 us (7%)
  local copies, waits for them, and re-layouts  26 us (4%)
  between operations  14.9 us (2%)
  starting transfers between devices  8.08 us (1%)
    reduce_scatter x4, waiting for transfers between devices, scatter(): lax.psum_scatter(partial.reshape(-1, partial.shape[-1]), axes, scatter_di...  280 us
    all_gather x1, waiting for transfers between devices, on_device(): full_inner = lax.all_gather(inner_weight, whole, axis=0, tiled=True)  60.4 us
    all_gather x1, waiting for transfers between devices, on_device(): full_outer = lax.all_gather(outer_weight.T, whole, axis=0, tiled=True)  55.4 us
    dot_general x21, matrix products, mix(): lax.dot_general(left, right, (dims, ((), ())), preferred_element_type=jnp...  52.6 us
    all_gather x1, waiting for transfers between devices, on_device(): summed = jnp.sum(lax.all_gather(block_here, ('dp', 'tensor')), axis=0)  21.7 us
    all_gather x1, waiting for transfers between devices, on_device(): lax.all_gather(jnp.concatenate([query_weight, key_weight, value_weight],...  21.4 us
    ppermute x1, waiting for transfers between devices, on_device(): lax.ppermute(lax.dynamic_slice_in_dim(partial_input, other_start, own_row...  18.6 us
    ppermute x1, waiting for transfers between devices, on_device(): other_tokens = lax.ppermute(tokens, 'tensor', swap)  16.1 us
  transfers between devices with their start and end apart: 13, of which 11 were waited for; matrix products, arithmetic and copies ran while one was open for 23% of the time, Pallas kernels for 0%

profile of v1, /device:TPU:0, one launch (start us, length us, event | category | flops | bytes accessed | tf_op | source)
XLA Modules:
  0.0 716.1 jit_solution(15956055230531033520)
XLA Ops:
  10.3 3.0 collective-permute-start
  14.9 16.1 %collective-permute-done = bf16[512,768]{1,0:T(8,128)(2,1)S(1)} collective-permute-done((bf16[512,768]{1,0:T(8,128)(2,1)}, bf16[512,768]{1,0:T(8,128)(2,1)S(1)}, u32[]{:S(2)}, u32[]{:S(2)}) %collective-permute-start) | collective-permute-done | bytes 786464 | tf_op jit(solution)/shard_map/ppermute | solution.py:159
  32.3 21.4 %all-gather.7.cloned.1.call-done = bf16[768,1152]{1,0:T(8,128)(2,1)} async-done(((bf16[48,1152]{1,0:T(8,128)(2,1)}), bf16[768,1152]{1,0:T(8,128)(2,1)}) %all-gather.7.cloned.1.call-update) | async-done | bytes 1769488 | tf_op jit(solution)/shard_map/all_gather | solution.py:160
  53.7 3.7 add_convert_fusion
  58.6 35.0 %while.47 = (s32[]{:T(128)}, bf16[2,512,6,64]{1,3,2,0:T(8,128)(2,1)S(1)}, f32[2,6,512]{2,1,0:T(8,128)S(1)}, s32[2]{0:T(128)S(1)}, s32[1024]{0:T(1024)S(1)}, /*in...) while((s32[]{:T(128)}, ...), condition=%wide.region_3.4_spmd, body=%wide.region_0.3_spmd.sunk | while | flops 842201600 | bytes 92672224 | solution.py:50
  61.4 2.4 fusion.143
  63.9 3.7 exponential_reduce_fusion.2
  68.4 7.8 %fusion.144 = bf16[2,512,6,64]{1,3,2,0:T(8,128)(2,1)S(1)} fusion(bf16[2,512,6,64]{1,3,2,0:T(8,128)(2,1)S(1)} %get-tuple-element.507, s32[]{:T(128)} %get-tuple-element.506, bf16[1024,6,64]{0,2,1:T(8,128)(2,1)S(1)} %get-tuple-element.527, f32[6,512,1024]{2,1,0:T(8,128)} %copy-done.2, f32[6,512]{1,0:T(8,128)S(1)} %get-tuple-element.477, ...), kind=kOutput, calls=%fused_computation.11.clone.1 | convolution fusion | flops 415432704 | bytes 14303236 | tf_op jit(solution)/shard_map/while/body/eval_jaxpr/while/body/eval_jaxpr/hqk,khd->qhd/dot_general | solution.py:45
  78.8 2.4 fusion.143
  81.3 3.7 exponential_reduce_fusion.2
  85.8 7.8 %fusion.144 = bf16[2,512,6,64]{1,3,2,0:T(8,128)(2,1)S(1)} fusion(bf16[2,512,6,64]{1,3,2,0:T(8,128)(2,1)S(1)} %get-tuple-element.507, s32[]{:T(128)} %get-tuple-element.506, bf16[1024,6,64]{0,2,1:T(8,128)(2,1)S(1)} %get-tuple-element.527, f32[6,512,1024]{2,1,0:T(8,128)} %copy-done.2, f32[6,512]{1,0:T(8,128)S(1)} %get-tuple-element.477, ...), kind=kOutput, calls=%fused_computation.11.clone.1 | convolution fusion | flops 415432704 | bytes 14303236 | tf_op jit(solution)/shard_map/while/body/eval_jaxpr/while/body/eval_jaxpr/hqk,khd->qhd/dot_general | solution.py:45
  95.5 1.9 copy.69
  100.2 9.4 %all-gather.9.cloned.1.call-done = bf16[1536,384]{1,0:T(8,128)(2,1)} async-done(((bf16[48,384]{1,0:T(8,128)(2,1)}), bf16[1536,384]{1,0:T(8,128)(2,1)}) %all-gather.9.cloned.1.call-update) | async-done | bytes 1179664 | tf_op jit(solution)/shard_map/all_gather | solution.py:163
  111.5 1.9 fusion.92
  115.7 60.4 %all-gather.11.cloned.1.call-done = bf16[1536,1536]{1,0:T(8,128)(2,1)} async-done(((bf16[48,1536]{1,0:T(8,128)(2,1)}), bf16[1536,1536]{1,0:T(8,128)(2,1)}) %all-gather.11.cloned.1.call-update) | async-done | bytes 4718608 | tf_op jit(solution)/shard_map/all_gather | solution.py:164
  176.2 5.8 multiply_convert_fusion.1
  182.0 3.5 multiply_convert_fusion.2
  185.5 55.4 %all-gather.13.cloned.1.call-done = bf16[1536,1536]{1,0:T(8,128)(2,1)} async-done(((bf16[48,1536]{1,0:T(8,128)(2,1)}), bf16[1536,1536]{1,0:T(8,128)(2,1)}) %all-gather.13.cloned.1.call-update) | async-done | bytes 4718608 | tf_op jit(solution)/shard_map/all_gather | solution.py:165
  240.9 3.7 fusion.54
  248.7 2.1 fusion.84
  250.9 3.2 convert_reduce_fusion.2
  254.1 3.2 convert_reduce_fusion.1
  258.7 2.3 multiply_reduce_fusion.1
  269.9 7.7 %collective-permute-done.2 = bf16[512,384]{1,0:T(8,128)(2,1)} collective-permute-done((bf16[512,384]{1,0:T(8,128)(2,1)}, bf16[512,384]{1,0:T(8,128)(2,1)}, u32[]{:S(2)}, u32[]{:S(2)}) %collective-permute-start.2) | collective-permute-done | bytes 393248 | tf_op jit(solution)/shard_map/ppermute | solution.py:236
  281.0 67.2 %while.48 = (s32[]{:T(128)}, f32[1024,6,64]{0,2,1:T(8,128)}, f32[1024,6,64]{0,2,1:T(8,128)}, bf16[2,512,6,64]{1,3,2,0:T(8,128)(2,1)}, s32[2]{0:T(128)S(1)}, /*in...) while((s32[]{:T(128)}, f32[1024,6,64]{0,2,1:T(8,128)}, ...), condition=%wide.region_14.15_spmd.clone, body=%wide.region_12.14_spmd.clone.sunk | while | flops 2064906752 | bytes 217293712 | solution.py:89
  286.0 6.3 multiply_reduce_fusion.7
  292.3 5.0 multiply_convert_fusion.4
  297.3 5.3 bitcast_add_fusion.4
  302.7 6.4 fusion.156
  309.1 4.8 bitcast_add_fusion.5
  316.6 1.8 fusion.154
  318.5 6.3 multiply_reduce_fusion.7
  324.8 5.0 multiply_convert_fusion.4
  329.9 5.7 bitcast_add_fusion.4
  335.6 6.3 fusion.156
  341.9 6.0 bitcast_add_fusion.5
  348.1 2.1 copy.67
  353.5 4.9 convolution_convert_fusion.4
  358.5 2.9 fusion.46
  362.9 2.5 pad_maximum_fusion.1
  366.5 2.9 fusion.44
  370.9 2.6 pad_maximum_fusion
  373.5 3.7 fusion.83
  378.8 18.6 %collective-permute-done.3 = bf16[512,768]{1,0:T(8,128)(2,1)S(1)} collective-permute-done((bf16[512,768]{1,0:T(8,128)(2,1)S(1)}, bf16[512,768]{1,0:T(8,128)(2,1)S(1)}, u32[]{:S(2)}, u32[]{:S(2)}) %collective-permute-start.3) | collective-permute-done | bytes 786464 | tf_op jit(solution)/shard_map/ppermute | solution.py:258
  400.3 21.7 %all-gather.15.cloned.1.call-done = f32[294912]{0:T(1024)} async-done(((f32[9216]{0:T(1024)}), f32[294912]{0:T(1024)}) %all-gather.15.cloned.1.call-update) | async-done | bytes 1179664 | tf_op jit(solution)/shard_map/all_gather | solution.py:293
  424.8 59.0 %reduce-scatter.5.cloned.1.call-done = bf16[48,1152]{1,0:T(8,128)(2,1)} async-done(((bf16[768,1152]{1,0:T(8,128)(2,1)}), bf16[48,1152]{1,0:T(8,128)(2,1)}) %reduce-scatter.5.cloned.1.call-update) | async-done | bytes 110608 | tf_op jit(solution)/shard_map/reduce_scatter | solution.py:268
  485.3 110.4 %reduce-scatter.11.cloned.1.call-done = bf16[48,1536]{1,0:T(8,128)(2,1)} async-done(((bf16[1536,1536]{1,0:T(8,128)(2,1)}), bf16[48,1536]{1,0:T(8,128)(2,1)}) %reduce-scatter.11.cloned.1.call-update) | async-done | bytes 147472 | tf_op jit(solution)/shard_map/reduce_scatter | solution.py:268
  597.3 110.4 %reduce-scatter.9.cloned.1.call-done = bf16[48,1536]{1,0:T(8,128)(2,1)} async-done(((bf16[1536,1536]{1,0:T(8,128)(2,1)}), bf16[48,1536]{1,0:T(8,128)(2,1)}) %reduce-scatter.9.cloned.1.call-update) | async-done | bytes 147472 | tf_op jit(solution)/shard_map/reduce_scatter | solution.py:268
  (244 shorter events, 64.3 us)
Async XLA Ops:
  7.2 46.5 %all-gather.7.cloned.1.call-start = ((), (), s32[]{:S(2)}) async-start(), calls=%async_computation.4 | async-start | bytes 1880064 | tf_op jit(solution)/shard_map/all_gather | solution.py:160
  8.7 100.9 %all-gather.9.cloned.1.call-start = ((), (), s32[]{:S(2)}) async-start(), calls=%async_computation.5 | async-start | bytes 1216512 | tf_op jit(solution)/shard_map/all_gather | solution.py:163
  9.5 166.7 %all-gather.11.cloned.1.call-start = ((), (), s32[]{:S(2)}) async-start(), calls=%async_computation.6 | async-start | bytes 4866048 | tf_op jit(solution)/shard_map/all_gather | solution.py:164
  10.2 230.7 %all-gather.13.cloned.1.call-start = ((), (), s32[]{:S(2)}) async-start(), calls=%async_computation.7 | async-start | bytes 4866048 | tf_op jit(solution)/shard_map/all_gather | solution.py:165
  10.3 20.8 %collective-permute-start = (bf16[512,768]{1,0:T(8,128)(2,1)}, bf16[512,768]{1,0:T(8,128)(2,1)S(1)}, u32[]{:S(2)}, u32[]{:S(2)}) collective-permute-start(bf16[512,768]{1,0:T(8,128)(2,1)} %param.23), channel_id=1, source_target_pairs={{0,1},{1,0},{2,3},{3,2},{4,5},{5,4},{6,7},{7,6},{8,9},{9,8},{10,11... | collective-permute-start | bytes 2359304 | tf_op jit(solution)/shard_map/ppermute | solution.py:159
  13.3 385.6 %reduce-scatter.7.cloned.1.call-start = ((), (), s32[]{:S(2)}) async-start(), calls=%async_computation.9 | async-start | bytes 1216512 | tf_op jit(solution)/shard_map/reduce_scatter | solution.py:268
  32.3 21.4 %copy-start.19 = (bf16[512,768]{1,0:T(8,128)(2,1)}, bf16[512,768]{1,0:T(8,128)(2,1)S(1)}, u32[]{:S(2)}) copy-start(bf16[512,768]{1,0:T(8,128)(2,1)S(1)} %get-tuple-element.315) | copy-start | bytes 2359300
  32.3 21.4 %copy-start.20 = (bf16[512,768]{1,0:T(8,128)(2,1)}, bf16[512,768]{1,0:T(8,128)(2,1)S(1)}, u32[]{:S(2)}) copy-start(bf16[512,768]{1,0:T(8,128)(2,1)S(1)} %get-tuple-element.316) | copy-start | bytes 2359300
  63.9 4.5 copy-start.2
  81.3 4.5 copy-start.2
  94.4 4.6 copy-start.26
  95.5 15.9 %copy-start.38 = (f32[768]{0:T(1024)S(1)}, f32[768]{0:T(1024)}, u32[]{:S(2)}) copy-start(f32[768]{0:T(1024)} %param.30) | copy-start | bytes 9220
  97.4 12.2 %collective-permute-start.1 = (bf16[512,384]{1,0:T(8,128)(2,1)}, bf16[512,384]{1,0:T(8,128)(2,1)S(1)}, u32[]{:S(2)}, u32[]{:S(2)}) collective-permute-start(bf16[512,384]{1,0:T(8,128)(2,1)} %copy.69), channel_id=1, source_target_pairs={{0,1},{1,0},{2,3},{3,2},{4,5},{5,4},{6,7},{7,6},{8,9},{9,8},{10,11... | collective-permute-start | bytes 1179656 | tf_op jit(solution)/shard_map/ppermute | solution.py:184
  111.4 3.1 copy-start.27
  111.4 3.1 copy-start.35
  176.2 5.8 copy-start.15
  176.2 5.8 copy-start.40
  240.9 3.7 copy-start.7
  240.9 4.0 copy-start.41
  240.9 4.0 copy-start.42
  240.9 4.4 copy-start.49
  250.9 3.2 copy-start.17
  250.9 3.2 copy-start.44
  250.9 6.3 slice-start
  254.1 4.6 copy-start.43
  254.1 3.2 slice-start.1
  262.1 3.9 copy-start.8
  264.5 3.5 copy-start.21
  266.0 11.6 %collective-permute-start.2 = (bf16[512,384]{1,0:T(8,128)(2,1)}, bf16[512,384]{1,0:T(8,128)(2,1)}, u32[]{:S(2)}, u32[]{:S(2)}) collective-permute-start(bf16[512,384]{1,0:T(8,128)(2,1)} %get-tuple-element.345), channel_id=1, source_target_pairs={{0,1},{1,0},{2,3},{3,2},{4,5},{5,4},{6,7},{7,6},{8,9},{9,8},{10,11... | collective-permute-start | bytes 1179656 | tf_op jit(solution)/shard_map/ppermute | solution.py:236
  268.7 8.9 %copy-start.22 = (bf16[512,384]{1,0:T(8,128)(2,1)S(1)}, bf16[512,384]{1,0:T(8,128)(2,1)}, u32[]{:S(2)}) copy-start(bf16[512,384]{1,0:T(8,128)(2,1)} %copy-done.21) | copy-start | bytes 1179652
  268.7 8.9 %copy-start.23 = (bf16[512,384]{1,0:T(8,128)(2,1)S(1)}, bf16[512,384]{1,0:T(8,128)(2,1)}, u32[]{:S(2)}) copy-start(bf16[512,384]{1,0:T(8,128)(2,1)} %get-tuple-element.346) | copy-start | bytes 1179652
  269.9 152.1 %all-gather.15.cloned.1.call-start = ((), (), s32[]{:S(2)}) async-start(), calls=%async_computation.12 | async-start | bytes 1216512 | tf_op jit(solution)/shard_map/all_gather | solution.py:293
  281.3 4.6 copy-start.4
  286.0 6.3 copy-start
  297.3 11.7 %copy-start.1 = (f32[6,512,1024]{2,1,0:T(8,128)S(1)}, f32[6,512,1024]{2,1,0:T(8,128)}, u32[]{:S(2)}) copy-start(f32[6,512,1024]{2,1,0:T(8,128)} %copy-done) | copy-start | bytes 37748740 | tf_op jit(solution)/shard_map/while/body/eval_jaxpr/while
  302.7 6.4 copy-start.10
  309.1 4.8 copy-start.5
  313.9 4.6 copy-start.4
  318.5 6.3 copy-start
  329.9 12.1 %copy-start.1 = (f32[6,512,1024]{2,1,0:T(8,128)S(1)}, f32[6,512,1024]{2,1,0:T(8,128)}, u32[]{:S(2)}) copy-start(f32[6,512,1024]{2,1,0:T(8,128)} %copy-done) | copy-start | bytes 37748740 | tf_op jit(solution)/shard_map/while/body/eval_jaxpr/while
  335.6 6.3 copy-start.10
  341.9 6.0 copy-start.5
  353.4 5.0 copy-start.18
  353.4 130.3 %reduce-scatter.5.cloned.1.call-start = ((), (), s32[]{:S(2)}) async-start(), calls=%async_computation.8 | async-start | bytes 1880064 | tf_op jit(solution)/shard_map/reduce_scatter | solution.py:268
  358.4 237.3 %reduce-scatter.11.cloned.1.call-start = ((), (), s32[]{:S(2)}) async-start(), calls=%async_computation.11 | async-start | bytes 4866048 | tf_op jit(solution)/shard_map/reduce_scatter | solution.py:268
  365.4 342.3 %reduce-scatter.9.cloned.1.call-start = ((), (), s32[]{:S(2)}) async-start(), calls=%async_computation.10 | async-start | bytes 4866048 | tf_op jit(solution)/shard_map/reduce_scatter | solution.py:268
  377.3 20.2 %copy-start.9 = (f32[512,768]{1,0:T(8,128)S(1)}, f32[512,768]{1,0:T(8,128)}, u32[]{:S(2)}) copy-start(f32[512,768]{1,0:T(8,128)} %copy-done.8) | copy-start | bytes 4718596
  377.4 20.1 %collective-permute-start.3 = (bf16[512,768]{1,0:T(8,128)(2,1)S(1)}, bf16[512,768]{1,0:T(8,128)(2,1)S(1)}, u32[]{:S(2)}, u32[]{:S(2)}) collective-permute-start(bf16[512,768]{1,0:T(8,128)(2,1)S(1)} %dynamic-slice_convert_fusion), channel_id=1, source_target_pairs={{0,1},{1,0},{2,3},{3,2},{4,5},{5,4},{6,7},{7,6},{8,9},{9,8},{10,11... | collective-permute-start | bytes 2359304 | tf_op jit(solution)/shard_map/ppermute | solution.py:258
  (23 other events, 44.3 us)
Sparse Core Ops, SparseCore 0:
  10.7 42.8 all-gather.6
  56.6 53.0 all-gather.8
  112.6 63.5 all-gather.10
  179.0 61.8 all-gather.12
  270.0 95.3 reduce-scatter.6
  368.8 53.1 all-gather.14
  425.8 57.9 reduce-scatter.4
  489.2 106.4 reduce-scatter.10
  601.2 106.4 reduce-scatter.8
